TPU v7x, 32 devices: a whole 2x2x4 slice. The times are simulated.
32 devices in a mesh: clip: 2 (over y), tm: 4 (over z), head: 2 (over x), sub: 2 (over core).
Axes of the slice: x: 2, y: 2, z: 4, core: 2. Of those that a mesh axis runs over, the one named last changes fastest.
Arguments:
- queries: bfloat16 [8, 256, 3072], P(('clip', 'tm'), None, ('head', 'sub')), parts along dimension 0, may hold values from -6 to 6, as said below
- keys: bfloat16 [8, 256, 3072], P(('clip', 'tm'), None, ('head', 'sub')), parts along dimension 0, may hold values from -6 to 6, as said below
- values: bfloat16 [8, 256, 3072], P(('clip', 'tm'), None, ('head', 'sub')), parts along dimension 0, may hold values from -6 to 6
- band_table: int32 [4, 4], replicated, may hold values from 0 to 3, as said below
- windows: int32 [7], replicated, may hold values from 1 to 128, as said below
- out_weight: bfloat16 [3072, 3072], P(('head', 'sub')), may hold values from -0.109375 to 0.109375
Outputs:
- mixed: bfloat16 [8, 256, 3072], P(('clip', 'tm'), ('head', 'sub')), parts along dimension 0
There are 2 independent parts, one for each index of `clip`. A program takes and returns all parts, laid end to end along the dimension named above; an argument that names none is the same for every part. Nothing has to cross between parts.
Inputs may be any that keep to these rules, and one draw needn't show every extreme that they name: `queries`: entries of normal law within the range; some rows may be aligned with some key rows. `keys`: entries of normal law within the range; some rows may be aligned with some query rows. `band_table`: Symmetric; 0 exactly on the diagonal; off the diagonal, for frames at distance d it is floor(log2 d) + 1 or one more, never above 6; the pair of frames 0 and 3 takes the one more (up to 6). windows[0] = 128; for k >= 1, windows[k] lies between max(1, 64 // 2**k) and max(that + 1, 128 // 2**k + 1) - 1.
All inputs are finite; a program needn't handle non-finite values.
Results may differ from a plain program's by a relative error of at most 0.015.
Values may be sent and summed in bfloat16 or wider, within the bound.
A program may use at most 64 MiB of HBM per device.

v0:
```python
import jax
import jax.numpy as jnp
from jax import lax
from jax.sharding import PartitionSpec as P

HEAD = 128


def local(queries, keys, values, band_table, windows, out_weight):
    frames, length, width = queries.shape
    heads = width // HEAD
    scale = HEAD ** (-0.5)
    here = lax.axis_index("tm") * frames
    query = queries[0].reshape(length, heads, HEAD)
    places = lax.iota(jnp.int32, length)
    gap = jnp.abs(places[:, None] - places[None, :])

    def absorb(carry, key_frame, value_frame, frame, usable):
        peak, total, numer = carry
        reach = windows[band_table[here, frame]]
        allowed = (gap <= reach)[None] & usable
        scores = (
            jnp.einsum(
                "phd,qhd->hpq",
                query,
                key_frame.reshape(length, heads, HEAD),
                preferred_element_type=jnp.float32,
            )
            * scale
        )
        masked = jnp.where(allowed, scores, jnp.float32(-1e30))
        top = jnp.maximum(peak, jnp.max(masked, axis=-1))
        weights = jnp.where(allowed, jnp.exp(scores - top[:, :, None]), jnp.float32(0.0))
        shrink = jnp.exp(peak - top)
        total = total * shrink + jnp.sum(weights, axis=-1)
        added = jnp.einsum(
            "hpq,qhd->phd",
            weights.astype(jnp.bfloat16),
            value_frame.reshape(length, heads, HEAD),
            preferred_element_type=jnp.float32,
        )
        numer = numer * jnp.transpose(shrink)[:, :, None] + added
        return (top, total, numer)

    carry = (
        jnp.full((heads, length), -1e30, jnp.float32),
        jnp.zeros((heads, length), jnp.float32),
        jnp.zeros((length, heads, HEAD), jnp.float32),
    )
    skipped = -1
    state = carry
    key_part = lax.all_gather(keys, "tm", axis=0, tiled=True)
    value_part = lax.all_gather(values, "tm", axis=0, tiled=True)

    def advance(inner, item):
        key_frame, value_frame, offset = item
        usable = jnp.abs(offset - here) > skipped
        return (absorb(inner, key_frame, value_frame, offset, usable), None)

    state, unused = lax.scan(
        advance, state, (key_part, value_part, lax.iota(jnp.int32, key_part.shape[0]))
    )
    carry = state
    peak, total, numer = carry
    attended = (
        (numer / jnp.transpose(total)[:, :, None]).astype(jnp.bfloat16).reshape(length, width)
    )
    mixed = lax.psum_scatter(
        jnp.dot(attended, out_weight, preferred_element_type=jnp.float32).astype(jnp.bfloat16),
        ("head", "sub"),
        scatter_dimension=0,
        tiled=True,
    )
    return mixed[None]


def solution(mesh):
    return jax.shard_map(
        local,
        mesh=mesh,
        in_specs=(
            P(("clip", "tm"), None, ("head", "sub")),
            P(("clip", "tm"), None, ("head", "sub")),
            P(("clip", "tm"), None, ("head", "sub")),
            P(),
            P(),
            P(("head", "sub"), None),
        ),
        out_specs=P(("clip", "tm"), ("head", "sub"), None),
        check_vma=False,
    )
```

profile of v0, /device:TPU:0, one launch (start us, length us, event | category | flops | bytes accessed | tf_op | source)
XLA Modules:
  0.0 169.9 jit_solution(7781933475861130219)
XLA Ops:
  6.5 0.7 all-gather.3.cloned.1.call-update
  8.1 1.2 copy.17
  9.3 0.9 copy.19
  10.2 38.5 %all-gather.3.cloned.1.call-done = bf16[4,256,768]{2,1,0:T(8,128)(2,1)} async-done(((bf16[1,256,768]{2,1,0:T(8,128)(2,1)}), bf16[4,256,768]{2,1,0:T(8,128)(2,1)}) %all-gather.3.cloned.1.call-update) | async-done | bytes 1572880 | tf_op jit(solution)/shard_map/all_gather | solution.py:52
  48.7 37.5 %all-gather.5.cloned.1.call-done = bf16[4,256,768]{2,1,0:T(8,128)(2,1)} async-done(((bf16[1,256,768]{2,1,0:T(8,128)(2,1)}), bf16[4,256,768]{2,1,0:T(8,128)(2,1)}) %all-gather.5.cloned.1.call-update) | async-done | bytes 1572880 | tf_op jit(solution)/shard_map/all_gather | solution.py:53
  86.2 45.1 %while.17 = (s32[]{:T(128)}, f32[6,256]{1,0:T(8,128)S(1)}, f32[6,256]{1,0:T(8,128)S(1)}, f32[256,6,128]{0,2,1:T(8,128)S(1)}, s32[4]{0:T(128)S(1)}, /*index=5*/s3...) while((s32[]{:T(128)}, f32[6,256]{1,0:T(8,128)S(1)}, ...), condition=%wide.region_3.4_spmd.clone, body=%wide.region_0.3_spmd.clone.sunk | while | flops 205726720 | bytes 10977591 | solution.py:60
  88.5 1.3 dynamic_slice.40
  92.9 0.7 fusion.35
  93.6 1.2 constant_dynamic-slice_fusion.3
  94.9 1.5 fusion.36
  99.7 1.3 dynamic_slice.40
  104.2 0.7 fusion.35
  104.9 1.2 constant_dynamic-slice_fusion.3
  106.2 1.5 fusion.36
  111.0 1.3 dynamic_slice.40
  115.4 0.7 fusion.35
  116.2 1.2 constant_dynamic-slice_fusion.3
  117.5 1.5 fusion.36
  122.3 1.3 dynamic_slice.40
  126.7 0.7 fusion.35
  127.4 1.2 constant_dynamic-slice_fusion.3
  128.8 1.4 fusion.36
  131.4 4.9 %convolution_convert_fusion = bf16[256,3072]{1,0:T(8,128)(2,1)} fusion(bf16[256,768]{0,1:T(8,128)(2,1)S(1)} %bitcast.62, bf16[768,3072]{1,0:T(8,128)(2,1)} %param.13), kind=kOutput, calls=%fused_computation.25 | convolution fusion | flops 1208745984 | bytes 6684672 | tf_op jit(solution)/shard_map/dot_general | solution.py:69
  136.3 27.0 %reduce-scatter.2.cloned.1.call-done = bf16[64,3072]{1,0:T(8,128)(2,1)} async-done(((bf16[256,3072]{1,0:T(8,128)(2,1)}), bf16[64,3072]{1,0:T(8,128)(2,1)}) %reduce-scatter.2.cloned.1.call-update) | async-done | bytes 393232 | tf_op jit(solution)/shard_map/reduce_scatter | solution.py:68
  (48 shorter events, 10.5 us)
Async XLA Ops:
  6.5 79.6 %copy-start = (s32[7]{0:T(128)S(1)}, s32[7]{0:T(128)}, u32[]{:S(2)}) copy-start(s32[7]{0:T(128)} %param.12) | copy-start | bytes 88
  6.5 42.1 %all-gather.3.cloned.1.call-start = ((), (), s32[]{:S(2)}) async-start(), calls=%async_computation.1 | async-start | bytes 1966080 | tf_op jit(solution)/shard_map/all_gather | solution.py:52
  7.3 78.9 %all-gather.5.cloned.1.call-start = ((), (), s32[]{:S(2)}) async-start(), calls=%async_computation.2 | async-start | bytes 1966080 | tf_op jit(solution)/shard_map/all_gather | solution.py:53
  8.0 155.3 %reduce-scatter.2.cloned.1.call-start = ((), (), s32[]{:S(2)}) async-start(), calls=%async_computation.3 | async-start | bytes 1966080 | tf_op jit(solution)/shard_map/reduce_scatter | solution.py:68
Sparse Core Ops, SparseCore 0:
  8.9 39.7 all-gather.2
  50.2 35.8 all-gather.4
  136.4 26.8 reduce-scatter.1
where the time goes:
time: 171 us; the launch traced here: 170 us
  waiting for transfers between devices  104 us (61%)
  local copies, waits for them, and re-layouts  18.4 us (11%)
  loops' own time  16.9 us (10%)
  between operations  13.2 us (8%)
  matrix products  12.8 us (7%)
  other arithmetic  4.12 us (2%)
    all_gather x1, waiting for transfers between devices, local(): key_part = lax.all_gather(keys, 'tm', axis=0, tiled=True)  38.5 us
    all_gather x1, waiting for transfers between devices, local(): value_part = lax.all_gather(values, 'tm', axis=0, tiled=True)  37.5 us
    reduce_scatter x1, waiting for transfers between devices, local(): lax.psum_scatter(jnp.dot(attended, out_weight, preferred_element_type=jnp...  27 us
    another operation x1, loops' own time, local(): lax.scan(advance, state, (key_part, value_part, lax.iota(jnp.int32, key_p...  16.9 us
    dynamic_slice x16, local copies, waits for them, and re-layouts, local(): lax.scan(advance, state, (key_part, value_part, lax.iota(jnp.int32, key_p...  8.4 us
    dynamic_slice x8, local copies, waits for them, and re-layouts, absorb(): reach = windows[band_table[here, frame]]  7.86 us
    dot_general x4, matrix products, absorb(): jnp.einsum('phd,qhd->hpq', query, key_frame.reshape(length, heads, HEAD),...  5.81 us
    dot_general x1, matrix products, local(): jnp.dot(attended, out_weight, preferred_element_type=jnp.float32)  4.92 us
  transfers between devices with their start and end apart: 3, of which 3 were waited for; matrix products, arithmetic and copies ran while one was open for 1% of the time, Pallas kernels for 0%

commit v1 on v0

--- a/solution.py
+++ b/solution.py
@@ -50,7 +50,12 @@
     skipped = -1
     state = carry
     key_part = lax.all_gather(keys, "tm", axis=0, tiled=True)
-    value_part = lax.all_gather(values, "tm", axis=0, tiled=True)
+    ring = [values]
+    for hop in range(3):
+        ring.append(lax.ppermute(ring[-1], "tm", [(dev, (dev + 1) % 4) for dev in range(4)]))
+    value_part = jnp.roll(
+        jnp.concatenate(ring[::-1], axis=0), (lax.axis_index("tm") + 1) * ring[0].shape[0], axis=0
+    )
 
     def advance(inner, item):
         key_frame, value_frame, offset = item

time: 171 us -> 149 us (0.87)
  waiting for transfers between devices: 104 us -> 75 us
  starting transfers between devices: 0.08 us -> 8.3 us
  local copies, waits for them, and re-layouts: 18.4 us -> 22.8 us
  matrix products: 12.8 us -> 8.84 us
    ppermute x0 -> x3, waiting for transfers between devices: none -> 47.8 us  [local(): lax.ppermute(ring[-1], 'tm', [(dev, (dev + 1) % 4) for dev in range(4)])]
    all_gather x1, waiting for transfers between devices: 38.5 us -> 0.01 us  [local(): key_part = lax.all_gather(keys, 'tm', axis=0, tiled=True)]
    all_gather x1 -> x0, waiting for transfers between devices: 37.5 us -> none  [local(): value_part = lax.all_gather(values, 'tm', axis=0, tiled=True)]
    ppermute x0 -> x3, starting transfers between devices: none -> 8.26 us  [local(): lax.ppermute(ring[-1], 'tm', [(dev, (dev + 1) % 4) for dev in range(4)])]
    dot_general x4, matrix products: 5.81 us -> 1.83 us  [absorb(): jnp.einsum('phd,qhd->hpq', query, key_frame.reshape(length, heads, HEAD),...]
    dynamic_slice x16, local copies, waits for them, and re-layouts: 8.4 us -> 11.3 us  [local(): lax.scan(advance, state, (key_part, value_part, lax.iota(jnp.int32, key_p...]
  transfers between devices with their start and end apart: 3 -> 5, of which waited for: 3 -> 4; matrix products, arithmetic and copies ran while one was open for 1% -> 3% of each run, Pallas kernels for 0% -> 0%
where the time goes in v1:
time: 149 us; the launch traced here: 148 us
  waiting for transfers between devices  75 us (50%)
  local copies, waits for them, and re-layouts  22.8 us (15%)
  loops' own time  16.1 us (11%)
  between operations  13.5 us (9%)
  matrix products  8.84 us (6%)
  starting transfers between devices  8.3 us (6%)
  other arithmetic  3.85 us (3%)
    ppermute x3, waiting for transfers between devices, local(): lax.ppermute(ring[-1], 'tm', [(dev, (dev + 1) % 4) for dev in range(4)])  47.8 us
    reduce_scatter x1, waiting for transfers between devices, local(): lax.psum_scatter(jnp.dot(attended, out_weight, preferred_element_type=jnp...  26.5 us
    another operation x1, loops' own time, local(): lax.scan(advance, state, (key_part, value_part, lax.iota(jnp.int32, key_p...  16.1 us
    dynamic_slice x16, local copies, waits for them, and re-layouts, local(): lax.scan(advance, state, (key_part, value_part, lax.iota(jnp.int32, key_p...  11.3 us
    ppermute x3, starting transfers between devices, local(): lax.ppermute(ring[-1], 'tm', [(dev, (dev + 1) % 4) for dev in range(4)])  8.26 us
    dynamic_slice x8, local copies, waits for them, and re-layouts, absorb(): reach = windows[band_table[here, frame]]  7.46 us
    dot_general x1, matrix products, local(): jnp.dot(attended, out_weight, preferred_element_type=jnp.float32)  4.92 us
  transfers between devices with their start and end apart: 5, of which 4 were waited for; matrix products, arithmetic and copies ran while one was open for 3% of the time, Pallas kernels for 0%

profile of v1, /device:TPU:0, one launch (start us, length us, event | category | flops | bytes accessed | tf_op | source)
XLA Modules:
  0.0 148.4 jit_solution(16508331547041042653)
XLA Ops:
  6.5 0.7 all-gather.2.cloned.1.call-update
  7.3 1.2 copy.22
  8.5 3.1 %collective-permute-start = (bf16[1,256,768]{1,2,0:T(8,128)(2,1)S(1)}, bf16[1,256,768]{1,2,0:T(8,128)(2,1)S(1)}, u32[]{:S(2)}, u32[]{:S(2)}) collective-permute-start(bf16[1,256,768]{1,2,0:T(8,128)(2,1)S(1)} %copy.22), channel_id=1, source_target_pairs={{0,4},{4,8},{8,12},{12,0},{1,5},{5,9},{9,13},{13,1},{2,6},{6,10},{... | collective-permute-start | bytes 1179656 | tf_op jit(solution)/shard_map/ppermute | solution.py:55
  11.6 11.2 %collective-permute-done = bf16[1,256,768]{1,2,0:T(8,128)(2,1)S(1)} collective-permute-done((bf16[1,256,768]{1,2,0:T(8,128)(2,1)S(1)}, bf16[1,256,768]{1,2,0:T(8,128)(2,1)S(1)}, u32[]{:S(2)}, u32[]{:S(2)}) %collective-permute-start) | collective-permute-done | bytes 393248 | tf_op jit(solution)/shard_map/ppermute | solution.py:55
  22.8 21.7 %collective-permute-done.1 = bf16[1,256,768]{1,2,0:T(8,128)(2,1)S(1)} collective-permute-done((bf16[1,256,768]{1,2,0:T(8,128)(2,1)S(1)}, bf16[1,256,768]{1,2,0:T(8,128)(2,1)S(1)}, u32[]{:S(2)}, u32[]{:S(2)}) %collective-permute-start.1) | collective-permute-done | bytes 393248 | tf_op jit(solution)/shard_map/ppermute | solution.py:55
  44.5 5.2 %collective-permute-start.2 = (bf16[1,256,768]{1,2,0:T(8,128)(2,1)S(1)}, bf16[1,256,768]{1,2,0:T(8,128)(2,1)S(1)}, u32[]{:S(2)}, u32[]{:S(2)}) collective-permute-start(bf16[1,256,768]{1,2,0:T(8,128)(2,1)S(1)} %collective-permute-done.1), channel_id=1, source_target_pairs={{0,4},{4,8},{8,12},{12,0},{1,5},{5,9},{9,13},{13,1},{2,6},{6,10},{... | collective-permute-start | bytes 1179656 | tf_op jit(solution)/shard_map/ppermute | solution.py:55
  49.6 1.2 copy.21
  51.0 14.9 %collective-permute-done.2 = bf16[1,256,768]{1,2,0:T(8,128)(2,1)S(1)} collective-permute-done((bf16[1,256,768]{1,2,0:T(8,128)(2,1)S(1)}, bf16[1,256,768]{1,2,0:T(8,128)(2,1)S(1)}, u32[]{:S(2)}, u32[]{:S(2)}) %collective-permute-start.2) | collective-permute-done | bytes 393248 | tf_op jit(solution)/shard_map/ppermute | solution.py:55
  66.2 1.3 constant_dynamic-slice_fusion.2
  67.5 42.5 %while.17 = (s32[]{:T(128)}, f32[6,256]{1,0:T(8,128)S(1)}, f32[6,256]{1,0:T(8,128)S(1)}, f32[256,6,128]{0,2,1:T(8,128)S(1)}, s32[4]{0:T(128)S(1)}, /*index=5*/s3...) while((s32[]{:T(128)}, f32[6,256]{1,0:T(8,128)S(1)}, ...), condition=%wide.region_3.4_spmd.clone, body=%wide.region_0.3_spmd.clone.sunk | while | flops 205726720 | bytes 10191163 | solution.py:65
  69.7 1.3 dynamic_slice.48
  74.5 1.0 constant_dynamic-slice_fusion.5
  76.2 1.0 constant_dynamic-slice_fusion.6
  80.4 1.3 dynamic_slice.48
  85.1 1.0 constant_dynamic-slice_fusion.5
  86.8 1.0 constant_dynamic-slice_fusion.6
  91.0 1.3 dynamic_slice.48
  95.8 1.0 constant_dynamic-slice_fusion.5
  97.4 1.0 constant_dynamic-slice_fusion.6
  101.6 1.3 dynamic_slice.48
  106.4 1.0 constant_dynamic-slice_fusion.5
  108.1 1.0 constant_dynamic-slice_fusion.6
  110.0 4.9 %convolution_convert_fusion = bf16[256,3072]{1,0:T(8,128)(2,1)} fusion(bf16[256,768]{0,1:T(8,128)(2,1)S(1)} %bitcast.62, bf16[768,3072]{1,0:T(8,128)(2,1)} %param.13), kind=kOutput, calls=%fused_computation.25 | convolution fusion | flops 1208745984 | bytes 6684672 | tf_op jit(solution)/shard_map/dot_general | solution.py:74
  115.0 26.5 %reduce-scatter.2.cloned.1.call-done = bf16[64,3072]{1,0:T(8,128)(2,1)} async-done(((bf16[256,3072]{1,0:T(8,128)(2,1)}), bf16[64,3072]{1,0:T(8,128)(2,1)}) %reduce-scatter.2.cloned.1.call-update) | async-done | bytes 393232 | tf_op jit(solution)/shard_map/reduce_scatter | solution.py:73
  (61 shorter events, 13.7 us)
Async XLA Ops:
  6.5 60.9 %all-gather.2.cloned.1.call-start = ((), (), s32[]{:S(2)}) async-start(), calls=%async_computation.1 | async-start | bytes 1966080 | tf_op jit(solution)/shard_map/all_gather | solution.py:52
  7.3 134.3 %reduce-scatter.2.cloned.1.call-start = ((), (), s32[]{:S(2)}) async-start(), calls=%async_computation.2 | async-start | bytes 1966080 | tf_op jit(solution)/shard_map/reduce_scatter | solution.py:73
  8.5 14.3 %collective-permute-start = (bf16[1,256,768]{1,2,0:T(8,128)(2,1)S(1)}, bf16[1,256,768]{1,2,0:T(8,128)(2,1)S(1)}, u32[]{:S(2)}, u32[]{:S(2)}) collective-permute-start(bf16[1,256,768]{1,2,0:T(8,128)(2,1)S(1)} %copy.22), channel_id=1, source_target_pairs={{0,4},{4,8},{8,12},{12,0},{1,5},{5,9},{9,13},{13,1},{2,6},{6,10},{... | collective-permute-start | bytes 1179656 | tf_op jit(solution)/shard_map/ppermute | solution.py:55
  22.8 21.7 %collective-permute-start.1 = (bf16[1,256,768]{1,2,0:T(8,128)(2,1)S(1)}, bf16[1,256,768]{1,2,0:T(8,128)(2,1)S(1)}, u32[]{:S(2)}, u32[]{:S(2)}) collective-permute-start(bf16[1,256,768]{1,2,0:T(8,128)(2,1)S(1)} %collective-permute-done), channel_id=1, source_target_pairs={{0,4},{4,8},{8,12},{12,0},{1,5},{5,9},{9,13},{13,1},{2,6},{6,10},{... | collective-permute-start | bytes 1179656 | tf_op jit(solution)/shard_map/ppermute | solution.py:55
  44.5 21.5 %collective-permute-start.2 = (bf16[1,256,768]{1,2,0:T(8,128)(2,1)S(1)}, bf16[1,256,768]{1,2,0:T(8,128)(2,1)S(1)}, u32[]{:S(2)}, u32[]{:S(2)}) collective-permute-start(bf16[1,256,768]{1,2,0:T(8,128)(2,1)S(1)} %collective-permute-done.1), channel_id=1, source_target_pairs={{0,4},{4,8},{8,12},{12,0},{1,5},{5,9},{9,13},{13,1},{2,6},{6,10},{... | collective-permute-start | bytes 1179656 | tf_op jit(solution)/shard_map/ppermute | solution.py:55
  66.0 1.4 copy-start
Sparse Core Ops, SparseCore 0:
  8.9 51.3 all-gather.1
  115.1 26.3 reduce-scatter.1
